TPU v7x, 128 devices: a whole 4x4x4 slice. The times are simulated.
128 devices in a mesh: grow: 8 (over x_lo, y), gcol: 16 (over z, x_hi, core).
Axes of the slice: x: 4 (x_hi: 2, x_lo: 2; x = x_hi * 2 + x_lo), y: 4, z: 4, core: 2. Of those that a mesh axis runs over, the one named last changes fastest.
Arguments:
- screened: bfloat16 [2, 16384, 16384], P(None, 'grow', 'gcol'), may hold values from -6 to 6
- elements: bfloat16 [2, 1024, 16384], P(None, None, ('grow', 'gcol')), may hold values from -0.046875 to 0.046875
- energy_grid: float32 [256], replicated, may hold values from -3 to 3
- band_index: int32 [256], replicated, may hold values from 0 to 255
- energy_index: int32 [4, 16], replicated, may hold values from 0 to 255
Outputs:
- sigma: float32 [2, 4, 16], replicated
All inputs are finite; a program needn't handle non-finite values.
Results may differ from a plain program's by a relative error of at most 0.0003.
Values may be sent and summed in bfloat16 or wider, within the bound.
No kernel may reach another device: no remote copies, remote signals or barrier semaphores. Data moves between devices by JAX's collectives and lax.ppermute only.
A program may use at most 128 MiB of HBM per device.

v0:
```python
import jax
import jax.numpy as jnp
from jax import lax
from jax.sharding import PartitionSpec as P


def spread(block, axis, source):
    block = jnp.where(lax.axis_index(axis) == source, block, jnp.zeros_like(block))
    return lax.psum(block, axis)


def weights(energy_grid, band_index, energy_index):
    points = lax.broadcasted_iota(jnp.int32, (1, energy_grid.shape[0]), 1)
    band_energy = jnp.sum(
        jnp.where(band_index[:, None] == points, energy_grid[None, :], 0.0), axis=-1
    )
    eval_energy = jnp.sum(
        jnp.where(energy_index[:, :, None] == points[None], energy_grid[None, None, :], 0.0),
        axis=-1,
    )
    offset = eval_energy[:, None, :] - band_energy[None, :, None]
    denom = offset * offset + 0.25
    return (offset / denom, -0.5 / denom)


def weigh(s_re, s_im, wre, wim):
    outer = wre.shape[0]
    summed = wre.shape[1]
    sre = s_re.reshape(outer, summed)[:, :, None]
    sim = s_im.reshape(outer, summed)[:, :, None]
    scale = summed ** (-0.5)
    out_re = scale * jnp.sum(wre * sre - wim * sim, axis=1)
    out_im = scale * jnp.sum(wre * sim + wim * sre, axis=1)
    return (out_re, out_im)


def local(screened, elements, energy_grid, band_index, energy_index):
    row_part = lax.all_gather(elements, "gcol", axis=2, tiled=True)
    ncol = screened.shape[2]
    place = lax.axis_index("gcol")
    half = lax.dynamic_slice_in_dim(row_part, place % 2 * ncol, ncol, 2)
    col_part = spread(half, "grow", place // 2)
    prod = jnp.einsum("mph,wgh->mpwg", col_part, screened, preferred_element_type=jnp.float32)
    yre = prod[0, :, 0] - prod[1, :, 1]
    yim = prod[1, :, 0] + prod[0, :, 1]
    rre = row_part[0].astype(jnp.float32)
    rim = row_part[1].astype(jnp.float32)
    s_re = jnp.sum(rre * yre + rim * yim, axis=-1)
    s_im = jnp.sum(rre * yim - rim * yre, axis=-1)
    wre, wim = weights(energy_grid, band_index, energy_index)
    total_re, total_im = lax.psum((s_re, s_im), ("grow", "gcol"))
    out_re, out_im = weigh(total_re, total_im, wre, wim)
    return jnp.stack([out_re, out_im])


def solution(mesh):
    in_specs = (P(None, "grow", "gcol"), P(None, None, ("grow", "gcol")), P(), P(), P())
    out_specs = P()
    return jax.shard_map(local, mesh=mesh, in_specs=in_specs, out_specs=out_specs, check_vma=False)
```

profile of v0, /device:TPU:1, one launch (start us, length us, event | category | flops | bytes accessed | tf_op | source)
XLA Modules:
  0.0 312.0 jit_solution(5005722360260161644)
XLA Ops:
  6.5 0.0 copy-start
  6.5 0.0 copy-start.1
  6.5 0.0 copy-start.2
  6.5 0.0 all-gather.2.cloned.1.call-start
  6.5 0.7 all-gather.2.cloned.1.call-update
  7.3 0.0 all-reduce.3.cloned.1.call-start
  7.3 83.3 %all-gather.2.cloned.1.call-done = bf16[2,1024,2048]{2,1,0:T(8,128)(2,1)} async-done(((bf16[2,1024,128]{2,1,0:T(8,128)(2,1)}), bf16[2,1024,2048]{2,1,0:T(8,128)(2,1)}) %all-gather.2.cloned.1.call-update) | async-done | bytes 8388624 | tf_op jit(solution)/shard_map/all_gather | solution.py:38
  90.6 5.4 %dynamic-slice_select_fusion = bf16[2,1024,1024]{2,1,0:T(8,128)(2,1)} fusion(bf16[2,1024,2048]{2,1,0:T(8,128)(2,1)} %all-gather.2.cloned.1.call-done, s32[]{:T(128)S(6)} %select_n.35, pred[]{:T(512)S(6)} %eq.37), kind=kLoop, calls=%fused_computation.17 | loop fusion | flops 2097152 | bytes 8388613 | tf_op jit(solution)/shard_map/jit(_where)/select_n | solution.py:8
  96.0 0.0 all-reduce.3.cloned.1.call-update
  96.0 0.0 copy-done
  96.1 0.0 copy-done.1
  96.1 0.2 select_reduce_fusion.1
  96.2 0.0 copy-done.2
  96.2 0.2 select_reduce_fusion
  96.4 102.1 %all-reduce.3.cloned.1.call-done = bf16[2,1024,1024]{2,1,0:T(8,128)(2,1)} async-done(((bf16[2,1024,1024]{2,1,0:T(8,128)(2,1)}), bf16[2,1024,1024]{2,1,0:T(8,128)(2,1)}) %all-reduce.3.cloned.1.call-update) | async-done | bytes 4194320 | tf_op jit(solution)/shard_map/psum | solution.py:9
  198.5 25.1 %fusion.6 = f32[2,1024,2,2048]{3,1,2,0:T(8,128)} fusion(bf16[2,2048,1024]{2,1,0:T(8,128)(2,1)} %param.5, bf16[2,1024,1024]{2,1,0:T(8,128)(2,1)} %all-reduce.3.cloned.1.call-done), kind=kOutput, calls=%fused_computation.12 | convolution fusion | flops 17179869184 | bytes 46137344 | tf_op jit(solution)/shard_map/mph,wgh->mpwg/dot_general | solution.py:43
  223.6 16.1 %fusion.1 = (f32[1024]{0:T(1024)S(1)}, f32[1024]{0:T(1024)S(1)}) fusion(bf16[2,1024,2048]{2,1,0:T(8,128)(2,1)} %all-gather.2.cloned.1.call-done, f32[2,1024,2,2048]{3,1,2,0:T(8,128)} %fusion.6), kind=kLoop, calls=%fused_computation.5 | loop fusion | flops 25163776 | bytes 41951232 | tf_op jit(solution)/shard_map/reduce_sum | solution.py:48
  239.7 64.7 %all-reduce = (f32[4,256]{1,0:T(4,128)S(1)}, f32[4,256]{1,0:T(4,128)S(1)}) all-reduce(f32[4,256]{1,0:T(4,128)S(1)} %mul.85, f32[4,256]{1,0:T(4,128)S(1)} %mul.80), channel_id=1, replica_groups=mesh['grow'=8,'gcol'=16] {'grow','gcol'}, use_global_device_ids=true, to_apply=%region_6.7 | all-reduce | flops 2048 | bytes 16384 | tf_op jit(solution)/shard_map/psum | solution.py:51
  304.4 0.2 subtract_reduce_fusion
  304.6 0.6 pad_maximum_fusion
  (3 shorter events, 0.0 us)
Async XLA Ops:
  6.5 89.5 %copy-start = (f32[256]{0:T(256)S(1)}, f32[256]{0:T(256)}, u32[]{:S(2)}) copy-start(f32[256]{0:T(256)} %param.7) | copy-start | bytes 3076
  6.5 89.5 %copy-start.1 = (s32[4,16]{1,0:T(4,128)S(1)}, s32[4,16]{1,0:T(4,128)}, u32[]{:S(2)}) copy-start(s32[4,16]{1,0:T(4,128)} %param.9) | copy-start | bytes 772
  6.5 89.7 %copy-start.2 = (s32[256]{0:T(256)S(1)}, s32[256]{0:T(256)}, u32[]{:S(2)}) copy-start(s32[256]{0:T(256)} %param.8) | copy-start | bytes 3076
  6.5 84.1 %all-gather.2.cloned.1.call-start = ((), (), s32[]{:S(2)}) async-start(), calls=%async_computation | async-start | bytes 8912896 | tf_op jit(solution)/shard_map/all_gather | solution.py:38
  7.3 191.2 %all-reduce.3.cloned.1.call-start = ((), (), s32[]{:S(2)}) async-start(), calls=%async_computation.1 | async-start | bytes 8388608 | tf_op jit(solution)/shard_map/psum | solution.py:9
Sparse Core Ops, SparseCore 0:
  9.7 80.8 all-gather.1
  96.2 102.2 all-reduce.2
where the time goes:
time: 312 us
  waiting for transfers between devices  186 us (60%)
  blocking collectives  64.7 us (21%)
  matrix products  25.1 us (8%)
  other arithmetic  22.6 us (7%)
  between operations  13.5 us (4%)
    psum x1, waiting for transfers between devices, spread(): return lax.psum(block, axis)  102 us
    all_gather x1, waiting for transfers between devices, local(): row_part = lax.all_gather(elements, 'gcol', axis=2, tiled=True)  83.3 us
    psum x1, blocking collectives, local(): total_re, total_im = lax.psum((s_re, s_im), ('grow', 'gcol'))  64.7 us
    dot_general x1, matrix products, local(): jnp.einsum('mph,wgh->mpwg', col_part, screened, preferred_element_type=jn...  25.1 us
    reduce_sum x1, other arithmetic, local(): s_re = jnp.sum(rre * yre + rim * yim, axis=-1)  16.1 us
  transfers between devices with their start and end apart: 2, of which 2 were waited for; matrix products, arithmetic and copies ran while one was open for 0% of the time, Pallas kernels for 0%

commit v1 on v0

--- a/solution.py
+++ b/solution.py
@@ -48,7 +48,7 @@
     s_re = jnp.sum(rre * yre + rim * yim, axis=-1)
     s_im = jnp.sum(rre * yim - rim * yre, axis=-1)
     wre, wim = weights(energy_grid, band_index, energy_index)
-    total_re, total_im = lax.psum((s_re, s_im), ("grow", "gcol"))
+    total_re, total_im = lax.psum(lax.psum((s_re, s_im), "grow"), "gcol")
     out_re, out_im = weigh(total_re, total_im, wre, wim)
     return jnp.stack([out_re, out_im])
 

time: 312 us -> 299 us (0.958)
  blocking collectives: 64.7 us -> 51.2 us
    psum x1 -> x2, blocking collectives: 64.7 us -> 51.2 us  [local(): total_re, total_im = lax.psum(lax.psum((s_re, s_im), 'grow'), 'gcol')]
where the time goes in v1:
time: 299 us
  waiting for transfers between devices  186 us (62%)
  blocking collectives  51.2 us (17%)
  matrix products  25.1 us (8%)
  other arithmetic  22.6 us (8%)
  between operations  13.5 us (5%)
    psum x1, waiting for transfers between devices, spread(): return lax.psum(block, axis)  102 us
    all_gather x1, waiting for transfers between devices, local(): row_part = lax.all_gather(elements, 'gcol', axis=2, tiled=True)  83.3 us
    psum x2, blocking collectives, local(): total_re, total_im = lax.psum(lax.psum((s_re, s_im), 'grow'), 'gcol')  51.2 us
    dot_general x1, matrix products, local(): jnp.einsum('mph,wgh->mpwg', col_part, screened, preferred_element_type=jn...  25.1 us
    reduce_sum x1, other arithmetic, local(): s_re = jnp.sum(rre * yre + rim * yim, axis=-1)  16.1 us
  transfers between devices with their start and end apart: 2, of which 2 were waited for; matrix products, arithmetic and copies ran while one was open for 0% of the time, Pallas kernels for 0%

profile of v1, /device:TPU:1, one launch (start us, length us, event | category | flops | bytes accessed | tf_op | source)
XLA Modules:
  0.0 298.6 jit_solution(445606657830071588)
XLA Ops:
  6.5 0.0 copy-start
  6.5 0.0 copy-start.1
  6.5 0.0 copy-start.2
  6.5 0.0 all-gather.2.cloned.1.call-start
  6.5 0.7 all-gather.2.cloned.1.call-update
  7.3 0.0 all-reduce.4.cloned.1.call-start
  7.3 83.3 %all-gather.2.cloned.1.call-done = bf16[2,1024,2048]{2,1,0:T(8,128)(2,1)} async-done(((bf16[2,1024,128]{2,1,0:T(8,128)(2,1)}), bf16[2,1024,2048]{2,1,0:T(8,128)(2,1)}) %all-gather.2.cloned.1.call-update) | async-done | bytes 8388624 | tf_op jit(solution)/shard_map/all_gather | solution.py:38
  90.6 5.4 %dynamic-slice_select_fusion = bf16[2,1024,1024]{2,1,0:T(8,128)(2,1)} fusion(bf16[2,1024,2048]{2,1,0:T(8,128)(2,1)} %all-gather.2.cloned.1.call-done, s32[]{:T(128)S(6)} %select_n.35, pred[]{:T(512)S(6)} %eq.37), kind=kLoop, calls=%fused_computation.17 | loop fusion | flops 2097152 | bytes 8388613 | tf_op jit(solution)/shard_map/jit(_where)/select_n | solution.py:8
  96.0 0.0 all-reduce.4.cloned.1.call-update
  96.0 0.0 copy-done
  96.1 0.0 copy-done.1
  96.1 0.2 select_reduce_fusion.1
  96.2 0.0 copy-done.2
  96.2 0.2 select_reduce_fusion
  96.4 102.1 %all-reduce.4.cloned.1.call-done = bf16[2,1024,1024]{2,1,0:T(8,128)(2,1)} async-done(((bf16[2,1024,1024]{2,1,0:T(8,128)(2,1)}), bf16[2,1024,1024]{2,1,0:T(8,128)(2,1)}) %all-reduce.4.cloned.1.call-update) | async-done | bytes 4194320 | tf_op jit(solution)/shard_map/psum | solution.py:9
  198.5 25.1 %fusion.6 = f32[2,1024,2,2048]{3,1,2,0:T(8,128)} fusion(bf16[2,2048,1024]{2,1,0:T(8,128)(2,1)} %param.5, bf16[2,1024,1024]{2,1,0:T(8,128)(2,1)} %all-reduce.4.cloned.1.call-done), kind=kOutput, calls=%fused_computation.12 | convolution fusion | flops 17179869184 | bytes 46137344 | tf_op jit(solution)/shard_map/mph,wgh->mpwg/dot_general | solution.py:43
  223.6 16.1 %fusion.1 = (f32[1024]{0:T(1024)S(1)}, f32[1024]{0:T(1024)S(1)}) fusion(bf16[2,1024,2048]{2,1,0:T(8,128)(2,1)} %all-gather.2.cloned.1.call-done, f32[2,1024,2,2048]{3,1,2,0:T(8,128)} %fusion.6), kind=kLoop, calls=%fused_computation.5 | loop fusion | flops 25163776 | bytes 41951232 | tf_op jit(solution)/shard_map/reduce_sum | solution.py:48
  239.7 13.3 %all-reduce.1 = (f32[1024]{0:T(1024)S(1)}, f32[1024]{0:T(1024)S(1)}) all-reduce(f32[1024]{0:T(1024)S(1)} %get-tuple-element.6, f32[1024]{0:T(1024)S(1)} %get-tuple-element.5), channel_id=1, replica_groups=mesh['grow'=8,'gcol'=16] {'grow'}, use_global_device_ids=true, to_apply=%region_7.8 | all-reduce | flops 2048 | bytes 16384 | tf_op jit(solution)/shard_map/psum | solution.py:51
  253.0 38.0 %all-reduce = (f32[4,256]{1,0:T(4,128)S(1)}, f32[4,256]{1,0:T(4,128)S(1)}) all-reduce(f32[4,256]{1,0:T(4,128)S(1)} %mul.85, f32[4,256]{1,0:T(4,128)S(1)} %mul.80), channel_id=1, replica_groups=mesh['grow'=8,'gcol'=16] {'gcol'}, use_global_device_ids=true, to_apply=%region_8.9 | all-reduce | flops 2048 | bytes 16384 | tf_op jit(solution)/shard_map/psum | solution.py:51
  291.0 0.2 subtract_reduce_fusion
  291.2 0.6 pad_maximum_fusion
  (3 shorter events, 0.0 us)
Async XLA Ops:
  6.5 89.5 %copy-start = (f32[256]{0:T(256)S(1)}, f32[256]{0:T(256)}, u32[]{:S(2)}) copy-start(f32[256]{0:T(256)} %param.7) | copy-start | bytes 3076
  6.5 89.5 %copy-start.1 = (s32[4,16]{1,0:T(4,128)S(1)}, s32[4,16]{1,0:T(4,128)}, u32[]{:S(2)}) copy-start(s32[4,16]{1,0:T(4,128)} %param.9) | copy-start | bytes 772
  6.5 89.7 %copy-start.2 = (s32[256]{0:T(256)S(1)}, s32[256]{0:T(256)}, u32[]{:S(2)}) copy-start(s32[256]{0:T(256)} %param.8) | copy-start | bytes 3076
  6.5 84.1 %all-gather.2.cloned.1.call-start = ((), (), s32[]{:S(2)}) async-start(), calls=%async_computation | async-start | bytes 8912896 | tf_op jit(solution)/shard_map/all_gather | solution.py:38
  7.3 191.2 %all-reduce.4.cloned.1.call-start = ((), (), s32[]{:S(2)}) async-start(), calls=%async_computation.1 | async-start | bytes 8388608 | tf_op jit(solution)/shard_map/psum | solution.py:9
Sparse Core Ops, SparseCore 0:
  9.7 80.8 all-gather.1
  96.2 102.2 all-reduce.3
